TPU v7x, 512 devices: a whole 4x4x16 slice. The times are simulated.
512 devices in a mesh: dp: 8 (over y, core), expert: 64 (over x, z).
Axes of the slice: x: 4, y: 4, z: 16, core: 2. Of those that a mesh axis runs over, the one named last changes fastest.
Arguments:
- layer_in: bfloat16 [2048, 4096], P('expert', 'dp'), may hold values from -6 to 6
- grad_out: bfloat16 [2048, 4096], P('expert', 'dp'), may hold values from -6 to 6
- gate_prob: float32 [2048, 8], P('expert'), may hold values from 0.05 to 0.6
- expert_ids: int32 [2048, 8], P('expert'), may hold values from 0 to 31, as said below
- replica_index: int32 [2048, 8], P('expert'), may hold values from 0 to 3, as said below
- slot_expert: int32 [64], replicated, may hold values from 0 to 31, as said below
- w_gate: bfloat16 [64, 4096, 1024], P('expert', None, 'dp')
- w_up: bfloat16 [64, 4096, 1024], P('expert', None, 'dp')
- w_down: bfloat16 [64, 1024, 4096], P('expert', 'dp')
Outputs:
- grad_in: bfloat16 [2048, 4096], P('expert', 'dp')
- grad_w_down: bfloat16 [64, 1024, 4096], P('expert', 'dp')
Inputs may be any that keep to these rules, and one draw needn't show every extreme that they name: `slot_expert`: every expert owns one run of consecutive slots, counted cyclically (slot 63 is followed by slot 0), of 1 to 4 slots; the runs cover all 64 slots. `expert_ids`: the 8 experts of one token are different. `replica_index`: each entry is below the number of slots of the expert of the same choice. Of the 32 tokens of one index of expert, at most 8 choices go to any one slot, and in every draw some slot receives exactly 8 from the tokens of every index of expert.
All inputs are finite; a program needn't handle non-finite values.
Results may differ from a plain program's by a relative error of at most 0.014.
Values may be sent and summed in bfloat16 or wider, within the bound.
No kernel may reach another device: no remote copies, remote signals or barrier semaphores. Data moves between devices by JAX's collectives and lax.ppermute only.
A program may use at most 64 MiB of HBM per device.

v0:
```python
import jax
import jax.numpy as jnp
from jax import lax
from jax.sharding import PartitionSpec as P

TOP = 8


def passed_along(value, axis, steps):
    count = lax.axis_size(axis)
    pairs = [(source, (source + steps) % count) for source in range(count)]
    return lax.ppermute(value, axis, pairs)


def body(
    layer_in, grad_out, gate_prob, expert_ids, replica_index, slot_expert, w_gate, w_up, w_down
):
    slots = lax.axis_size("expert")
    maxrep = min(4, slots // 8)
    tok_count = layer_in.shape[0]
    capacity = tok_count // maxrep
    recv_rows = slots * capacity
    expert_count = (8 - maxrep) * slots // 8
    slot_index = jnp.arange(slots, dtype=jnp.int32)
    expert_index = jnp.arange(expert_count, dtype=jnp.int32)
    is_start = slot_expert != jnp.roll(slot_expert, 1)
    first_slot = jnp.sum(
        jnp.where(
            (slot_expert[None, :] == expert_index[:, None]) & is_start[None, :],
            slot_index[None, :],
            0,
        ),
        axis=1,
    )
    expert_flat = expert_ids.reshape(-1)
    route_slot = jnp.sum(
        jnp.where(expert_flat[:, None] == expert_index[None, :], first_slot[None, :], 0), axis=1
    )
    route_slot = (route_slot + replica_index.reshape(-1)) % slots
    onehot = (route_slot[:, None] == slot_index[None, :]).astype(jnp.int32)
    rank_in_slot = jnp.sum((jnp.cumsum(onehot, axis=0) - onehot) * onehot, axis=1)
    position = route_slot * capacity + rank_in_slot
    prob_flat = gate_prob.reshape(-1)

    def pack(values):
        buffer = jnp.zeros((recv_rows, values.shape[1]), values.dtype).at[position].set(values)
        return buffer.reshape(slots, capacity, values.shape[1])

    repeated = jnp.repeat(grad_out, TOP, axis=0).astype(jnp.float32)
    inputs, scaled = (
        lax.all_gather(
            lax.all_to_all(
                pack(jnp.repeat(layer_in, TOP, axis=0)),
                "expert",
                split_axis=0,
                concat_axis=0,
                tiled=True,
            ),
            "dp",
            axis=2,
            tiled=True,
        ),
        lax.all_gather(
            lax.all_to_all(
                pack((prob_flat[:, None] * repeated).astype(jnp.bfloat16)),
                "expert",
                split_axis=0,
                concat_axis=0,
                tiled=True,
            ),
            "dp",
            axis=2,
            tiled=True,
        ),
    )
    inputs = inputs.reshape(recv_rows, -1)
    scaled = scaled.reshape(recv_rows, -1)
    width = inputs.shape[1]
    gate_matrix = w_gate[0]
    up_matrix = w_up[0]
    down_matrix = w_down[0]
    gate_pre = jnp.dot(inputs, gate_matrix, preferred_element_type=jnp.float32)
    up_pre = jnp.dot(inputs, up_matrix, preferred_element_type=jnp.float32)
    hidden = (jax.nn.silu(gate_pre) * up_pre).astype(jnp.bfloat16)
    slot_partial = lax.dot_general(
        hidden, scaled, (((0,), (0,)), ((), ())), preferred_element_type=jnp.float32
    ).astype(jnp.bfloat16)
    slot_partial, scaled = lax.optimization_barrier((slot_partial, scaled))
    contract_last = (((1,), (1,)), ((), ()))
    hidden_grad = lax.dot_general(
        scaled, down_matrix, contract_last, preferred_element_type=jnp.float32
    )
    sigma = jax.nn.sigmoid(gate_pre)
    gate_grad = (hidden_grad * up_pre * sigma * (1.0 + gate_pre * (1.0 - sigma))).astype(
        jnp.bfloat16
    )
    up_grad = (hidden_grad * gate_pre * sigma).astype(jnp.bfloat16)
    partial_value = lax.dot_general(
        gate_grad, gate_matrix, contract_last, preferred_element_type=jnp.float32
    )
    partial_value = partial_value + lax.dot_general(
        up_grad, up_matrix, contract_last, preferred_element_type=jnp.float32
    )
    partial_value = partial_value.reshape(slots, capacity, width)
    summed = lax.psum_scatter(
        partial_value.astype(jnp.bfloat16), "dp", scatter_dimension=2, tiled=True
    ).astype(jnp.float32)
    returned = lax.all_to_all(
        summed.astype(jnp.bfloat16), "expert", split_axis=0, concat_axis=0, tiled=True
    ).astype(summed.dtype)
    flat_back = returned.reshape(recv_rows, -1)
    grad_in = jnp.sum(flat_back[position].reshape(tok_count, TOP, -1), axis=1).astype(jnp.bfloat16)
    own_index = lax.axis_index("expert")
    expert_here = jnp.sum(jnp.where(slot_index == own_index, slot_expert, 0))

    def same_at(offset):
        neighbour = (own_index - offset) % slots
        match = jnp.any((slot_index == neighbour) & (slot_expert == expert_here))
        return match.astype(jnp.float32)

    own = slot_partial.astype(jnp.float32)
    left = own + same_at(1) * passed_along(slot_partial, "expert", 1).astype(jnp.float32)
    right = own + same_at(-1) * passed_along(slot_partial, "expert", -1).astype(jnp.float32)
    far_left = passed_along(left.astype(jnp.bfloat16), "expert", 2).astype(jnp.float32)
    far_right = passed_along(right.astype(jnp.bfloat16), "expert", -2).astype(jnp.float32)
    total = left + same_at(2) * far_left + (right - own) + same_at(-2) * far_right
    grad_w_down = total.astype(jnp.bfloat16)[None]
    return (grad_in, grad_w_down)


def solution(mesh):
    placed = (
        P("expert", "dp"),
        P("expert", "dp"),
        P("expert", None),
        P("expert", None),
        P("expert", None),
        P(),
        P("expert", None, "dp"),
        P("expert", None, "dp"),
        P("expert", "dp", None),
    )
    return jax.shard_map(
        body,
        mesh=mesh,
        in_specs=placed,
        out_specs=(P("expert", "dp"), P("expert", "dp", None)),
        check_vma=False,
    )
```

profile of v0, /device:TPU:6, one launch (start us, length us, event | category | flops | bytes accessed | tf_op | source)
XLA Modules:
  0.0 280.3 jit_solution(15586533807323691807)
XLA Ops:
  7.2 0.8 copy.18
  8.1 0.1 reshape.135
  8.2 0.1 reshape.134
  8.3 0.1 reshape.133
  8.4 1.2 slice.14
  9.6 1.3 fusion.41
  10.9 2.1 broadcast_compare_fusion
  13.0 0.8 select_reduce_fusion.1
  13.8 0.8 copy.17
  14.5 0.1 eq.98
  14.6 0.1 select_reduce_fusion
  14.7 0.6 reduce-window.6
  15.4 0.2 slice_reduce_fusion
  15.6 0.1 fusion.33
  15.7 1.9 scatter_custom_fusion
  17.6 50.4 %all_to_all.15 = bf16[64,8,512]{2,1,0:T(8,128)(2,1)} all-to-all(bf16[64,8,512]{2,1,0:T(8,128)(2,1)S(1)} %bitcast.69), channel_id=1, replica_groups=mesh['dp'=8,'expert'=64] {'expert'}, dimensions={0} | all-to-all | bytes 1048576 | tf_op jit(solution)/shard_map/all_to_all | solution.py:52
  68.0 0.0 all-gather.5.cloned.1.call-start
  68.1 0.1 copy.22
  68.2 0.1 mul.80
  68.3 1.7 scatter_custom_fusion.1
  70.0 37.4 %all_to_all.16 = bf16[64,8,512]{2,1,0:T(8,128)(2,1)} all-to-all(bf16[64,8,512]{2,1,0:T(8,128)(2,1)S(1)} %bitcast.70), channel_id=1, replica_groups=mesh['dp'=8,'expert'=64] {'expert'}, dimensions={0} | all-to-all | bytes 1048576 | tf_op jit(solution)/shard_map/all_to_all | solution.py:64
  107.5 3.6 %fusion.3 = f32[512,128]{1,0:T(8,128)S(1)} fusion(bf16[64,8,4096]{2,1,0:T(8,128)(2,1)} %all-gather.3.cloned.1.call-done, bf16[1,4096,128]{2,1,0:T(8,128)(2,1)S(1)} %copy-done), kind=kOutput, calls=%fused_computation.8 | convolution fusion | flops 536870912 | bytes 5505024 | tf_op jit(solution)/shard_map/dot_general | solution.py:82
  111.1 0.1 copy-done.1
  111.2 2.0 fusion.1
  113.1 29.3 %all-gather.5.cloned.1.call-done = bf16[64,8,4096]{2,1,0:T(8,128)(2,1)} async-done(((bf16[64,8,512]{2,1,0:T(8,128)(2,1)}), bf16[64,8,4096]{2,1,0:T(8,128)(2,1)}) %all-gather.5.cloned.1.call-update) | async-done | bytes 4194320 | tf_op jit(solution)/shard_map/all_gather | solution.py:63
  142.5 3.2 %convolution_convert_fusion = bf16[128,4096]{1,0:T(8,128)(2,1)S(1)} fusion(f32[512,128]{1,0:T(8,128)} %fusion.1, f32[512,128]{1,0:T(8,128)S(1)} %fusion.3, bf16[64,8,4096]{2,1,0:T(8,128)(2,1)} %all-gather.5.cloned.1.call-done), kind=kOutput, calls=%fused_computation.5 | convolution fusion | flops 537788416 | bytes 5767168 | tf_op jit(solution)/shard_map/dot_general | solution.py:85
  145.7 0.3 copy-done.2
  146.0 0.3 copy-done.5
  146.3 1.2 fusion.10
  147.6 1.3 fusion.14
  148.8 3.2 %fusion = bf16[64,8,4096]{2,1,0:T(8,128)(2,1)} fusion(f32[512,4096]{1,0:T(8,128)S(1)} %fusion.14, bf16[1,4096,128]{2,1,0:T(8,128)(2,1)S(1)} %copy-done.3, f32[512,128]{1,0:T(8,128)S(1)} %fusion.10, f32[512,128]{1,0:T(8,128)S(1)} %fusion.3), kind=kOutput, calls=%fused_computation.4 | convolution fusion | flops 541458432 | bytes 14155776 | tf_op jit(solution)/shard_map/dot_general | solution.py:101
  152.1 3.6 %collective-permute-start = (bf16[128,4096]{1,0:T(8,128)(2,1)S(1)}, bf16[128,4096]{1,0:T(8,128)(2,1)S(1)}, u32[]{:S(2)}, u32[]{:S(2)}) collective-permute-start(bf16[128,4096]{1,0:T(8,128)(2,1)S(1)} %convolution_convert_fusion), channel_id=1, source_target_pairs={{0,1},{1,2},{2,3},{3,4},{4,5},{5,6},{6,7},{7,8},{8,9},{9,10},{10,1... | collective-permute-start | bytes 3145736 | tf_op jit(solution)/shard_map/ppermute | solution.py:12
  155.7 4.7 %collective-permute-start.2 = (bf16[128,4096]{1,0:T(8,128)(2,1)S(1)}, bf16[128,4096]{1,0:T(8,128)(2,1)}, u32[]{:S(2)}, u32[]{:S(2)}) collective-permute-start(bf16[128,4096]{1,0:T(8,128)(2,1)S(1)} %convolution_convert_fusion), channel_id=1, source_target_pairs={{0,63},{1,0},{2,1},{3,2},{4,3},{5,4},{6,5},{7,6},{8,7},{9,8},{10,9... | collective-permute-start | bytes 3145736 | tf_op jit(solution)/shard_map/ppermute | solution.py:12
  160.5 0.7 and_reduce_fusion.2
  162.5 19.4 %collective-permute-done = bf16[128,4096]{1,0:T(8,128)(2,1)S(1)} collective-permute-done((bf16[128,4096]{1,0:T(8,128)(2,1)S(1)}, bf16[128,4096]{1,0:T(8,128)(2,1)S(1)}, u32[]{:S(2)}, u32[]{:S(2)}) %collective-permute-start) | collective-permute-done | bytes 1048608 | tf_op jit(solution)/shard_map/ppermute | solution.py:12
  181.9 1.4 collective-permute-done.2
  183.2 3.2 %fusion.9 = (bf16[128,4096]{1,0:T(8,128)(2,1)}, bf16[128,4096]{1,0:T(8,128)(2,1)}) fusion(bf16[128,4096]{1,0:T(8,128)(2,1)S(1)} %collective-permute-done, bf16[128,4096]{1,0:T(8,128)(2,1)S(1)} %convolution_convert_fusion, f32[]{:T(128)S(6)} %convert_element_type.90, bf16[128,4096]{1,0:T(8,128)(2,1)} %collective-permute-done.2, f32[]{:T(128)S(6)} %convert_element_type.95), kind=kLoop, calls=%fused_computation.17 | loop fusion | flops 4718592 | bytes 5242888 | tf_op jit(solution)/shard_map/convert_element_type | solution.py:124
  186.4 5.0 %collective-permute-start.1 = (bf16[128,4096]{1,0:T(8,128)(2,1)}, bf16[128,4096]{1,0:T(8,128)(2,1)}, u32[]{:S(2)}, u32[]{:S(2)}) collective-permute-start(bf16[128,4096]{1,0:T(8,128)(2,1)} %get-tuple-element.10), channel_id=1, source_target_pairs={{0,2},{1,3},{2,4},{3,5},{4,6},{5,7},{6,8},{7,9},{8,10},{9,11},{10,... | collective-permute-start | bytes 3145736 | tf_op jit(solution)/shard_map/ppermute | solution.py:12
  191.4 3.9 %collective-permute-start.3 = (bf16[128,4096]{1,0:T(8,128)(2,1)}, bf16[128,4096]{1,0:T(8,128)(2,1)}, u32[]{:S(2)}, u32[]{:S(2)}) collective-permute-start(bf16[128,4096]{1,0:T(8,128)(2,1)} %get-tuple-element.11), channel_id=1, source_target_pairs={{0,62},{1,63},{2,0},{3,1},{4,2},{5,3},{6,4},{7,5},{8,6},{9,7},{10,... | collective-permute-start | bytes 3145736 | tf_op jit(solution)/shard_map/ppermute | solution.py:12
  195.3 2.9 %reduce-scatter.2.cloned.1.call-done = bf16[64,8,512]{2,1,0:T(8,128)(2,1)} async-done(((bf16[64,8,4096]{2,1,0:T(8,128)(2,1)}), bf16[64,8,512]{2,1,0:T(8,128)(2,1)}) %reduce-scatter.2.cloned.1.call-update) | async-done | bytes 524304 | tf_op jit(solution)/shard_map/reduce_scatter | solution.py:105
  198.1 16.4 %all-to-all-start.2 = ((bf16[64,8,512]{2,1,0:T(8,128)(2,1)}), bf16[64,8,512]{2,1,0:T(8,128)(2,1)}, u32[]{:S(2)}, u32[]{:S(2)}) async-start(bf16[64,8,512]{2,1,0:T(8,128)(2,1)} %reduce-scatter.2.cloned.1.call-done), calls=%async_computation.3 | async-start | bytes 1048576 | tf_op jit(solution)/shard_map/all_to_all | solution.py:108
  215.9 7.9 %collective-permute-done.1 = bf16[128,4096]{1,0:T(8,128)(2,1)} collective-permute-done((bf16[128,4096]{1,0:T(8,128)(2,1)}, bf16[128,4096]{1,0:T(8,128)(2,1)}, u32[]{:S(2)}, u32[]{:S(2)}) %collective-permute-start.1) | collective-permute-done | bytes 1048608 | tf_op jit(solution)/shard_map/ppermute | solution.py:12
  223.8 22.4 %collective-permute-done.3 = bf16[128,4096]{1,0:T(8,128)(2,1)} collective-permute-done((bf16[128,4096]{1,0:T(8,128)(2,1)}, bf16[128,4096]{1,0:T(8,128)(2,1)}, u32[]{:S(2)}, u32[]{:S(2)}) %collective-permute-start.3) | collective-permute-done | bytes 1048608 | tf_op jit(solution)/shard_map/ppermute | solution.py:12
  246.2 3.9 %fusion.17 = bf16[1,128,4096]{2,1,0:T(8,128)(2,1)} fusion(bf16[128,4096]{1,0:T(8,128)(2,1)} %collective-permute-done.3, f32[]{:T(128)S(6)} %convert_element_type.97, bf16[128,4096]{1,0:T(8,128)(2,1)} %collective-permute-done.2, f32[]{:T(128)S(6)} %convert_element_type.95, bf16[128,4096]{1,0:T(8,128)(2,1)} %collective-permute-done.1, ...), kind=kLoop, calls=%fused_computation.25 | loop fusion | flops 8388608 | bytes 6291472 | tf_op jit(solution)/shard_map/broadcast_in_dim | solution.py:127
  250.1 20.8 %all-to-all-done.2 = bf16[64,8,512]{2,1,0:T(8,128)(2,1)} async-done(((bf16[64,8,512]{2,1,0:T(8,128)(2,1)}), bf16[64,8,512]{2,1,0:T(8,128)(2,1)}, u32[]{:S(2)}, u32[]{:S(2)}) %all-to-all-start.2) | async-done | bytes 524320 | tf_op jit(solution)/shard_map/all_to_all | solution.py:108
  270.9 1.2 bitcast_convert_fusion
  272.1 1.0 gather_fusion
  273.0 0.7 bitcast_reduce_fusion
  (27 shorter events, 0.3 us)
Async XLA Ops:
  7.2 100.3 %copy-start = (bf16[1,4096,128]{2,1,0:T(8,128)(2,1)S(1)}, bf16[1,4096,128]{2,1,0:T(8,128)(2,1)}, u32[]{:S(2)}) copy-start(bf16[1,4096,128]{2,1,0:T(8,128)(2,1)} %param.15) | copy-start | bytes 3145732
  7.2 60.9 %copy-start.6 = (bf16[32,512]{1,0:T(8,128)(2,1)S(1)}, bf16[32,512]{1,0:T(8,128)(2,1)}, u32[]{:S(2)}) copy-start(bf16[32,512]{1,0:T(8,128)(2,1)} %param.10) | copy-start | bytes 98308
  7.2 60.9 %copy-start.7 = (f32[32,8]{0,1:T(8,128)S(1)}, f32[32,8]{0,1:T(8,128)}, u32[]{:S(2)}) copy-start(f32[32,8]{0,1:T(8,128)} %param.11) | copy-start | bytes 3076
  7.2 100.3 %all-gather.3.cloned.1.call-start = ((), (), s32[]{:S(2)}) async-start(), calls=%async_computation.4 | async-start | bytes 4718592 | tf_op jit(solution)/shard_map/all_gather | solution.py:51
  68.0 74.5 %all-gather.5.cloned.1.call-start = ((), (), s32[]{:S(2)}) async-start(), calls=%async_computation.5 | async-start | bytes 4718592 | tf_op jit(solution)/shard_map/all_gather | solution.py:63
  107.4 3.7 %copy-start.3 = (bf16[1,4096,128]{2,1,0:T(8,128)(2,1)S(1)}, bf16[1,4096,128]{2,1,0:T(8,128)(2,1)}, u32[]{:S(2)}) copy-start(bf16[1,4096,128]{2,1,0:T(8,128)(2,1)} %param.16) | copy-start | bytes 3145732
  107.4 90.7 %reduce-scatter.2.cloned.1.call-start = ((), (), s32[]{:S(2)}) async-start(), calls=%async_computation.6 | async-start | bytes 4718592 | tf_op jit(solution)/shard_map/reduce_scatter | solution.py:105
  107.5 3.7 %copy-start.1 = (bf16[64,8,4096]{2,1,0:T(8,128)(2,1)S(1)}, bf16[64,8,4096]{2,1,0:T(8,128)(2,1)}, u32[]{:S(2)}) copy-start(bf16[64,8,4096]{2,1,0:T(8,128)(2,1)} %all-gather.3.cloned.1.call-done) | copy-start | bytes 12582916
  142.5 3.5 %copy-start.2 = (bf16[64,8,4096]{2,1,0:T(8,128)(2,1)S(1)}, bf16[64,8,4096]{2,1,0:T(8,128)(2,1)}, u32[]{:S(2)}) copy-start(bf16[64,8,4096]{2,1,0:T(8,128)(2,1)} %all-gather.5.cloned.1.call-done) | copy-start | bytes 12582916
  142.5 3.8 %copy-start.5 = (bf16[1,128,4096]{2,1,0:T(8,128)(2,1)S(1)}, bf16[1,128,4096]{2,1,0:T(8,128)(2,1)}, u32[]{:S(2)}) copy-start(bf16[1,128,4096]{2,1,0:T(8,128)(2,1)} %param.17) | copy-start | bytes 3145732
  146.3 1.3 copy-start.4
  152.1 29.8 %collective-permute-start = (bf16[128,4096]{1,0:T(8,128)(2,1)S(1)}, bf16[128,4096]{1,0:T(8,128)(2,1)S(1)}, u32[]{:S(2)}, u32[]{:S(2)}) collective-permute-start(bf16[128,4096]{1,0:T(8,128)(2,1)S(1)} %convolution_convert_fusion), channel_id=1, source_target_pairs={{0,1},{1,2},{2,3},{3,4},{4,5},{5,6},{6,7},{7,8},{8,9},{9,10},{10,1... | collective-permute-start | bytes 3145736 | tf_op jit(solution)/shard_map/ppermute | solution.py:12
  155.7 27.5 %collective-permute-start.2 = (bf16[128,4096]{1,0:T(8,128)(2,1)S(1)}, bf16[128,4096]{1,0:T(8,128)(2,1)}, u32[]{:S(2)}, u32[]{:S(2)}) collective-permute-start(bf16[128,4096]{1,0:T(8,128)(2,1)S(1)} %convolution_convert_fusion), channel_id=1, source_target_pairs={{0,63},{1,0},{2,1},{3,2},{4,3},{5,4},{6,5},{7,6},{8,7},{9,8},{10,9... | collective-permute-start | bytes 3145736 | tf_op jit(solution)/shard_map/ppermute | solution.py:12
  186.4 37.4 %collective-permute-start.1 = (bf16[128,4096]{1,0:T(8,128)(2,1)}, bf16[128,4096]{1,0:T(8,128)(2,1)}, u32[]{:S(2)}, u32[]{:S(2)}) collective-permute-start(bf16[128,4096]{1,0:T(8,128)(2,1)} %get-tuple-element.10), channel_id=1, source_target_pairs={{0,2},{1,3},{2,4},{3,5},{4,6},{5,7},{6,8},{7,9},{8,10},{9,11},{10,... | collective-permute-start | bytes 3145736 | tf_op jit(solution)/shard_map/ppermute | solution.py:12
  191.4 54.8 %collective-permute-start.3 = (bf16[128,4096]{1,0:T(8,128)(2,1)}, bf16[128,4096]{1,0:T(8,128)(2,1)}, u32[]{:S(2)}, u32[]{:S(2)}) collective-permute-start(bf16[128,4096]{1,0:T(8,128)(2,1)} %get-tuple-element.11), channel_id=1, source_target_pairs={{0,62},{1,63},{2,0},{3,1},{4,2},{5,3},{6,4},{7,5},{8,6},{9,7},{10,... | collective-permute-start | bytes 3145736 | tf_op jit(solution)/shard_map/ppermute | solution.py:12
  198.1 72.8 %all-to-all-start.2 = ((bf16[64,8,512]{2,1,0:T(8,128)(2,1)}), bf16[64,8,512]{2,1,0:T(8,128)(2,1)}, u32[]{:S(2)}, u32[]{:S(2)}) async-start(bf16[64,8,512]{2,1,0:T(8,128)(2,1)} %reduce-scatter.2.cloned.1.call-done), calls=%async_computation.3 | async-start | bytes 1048576 | tf_op jit(solution)/shard_map/all_to_all | solution.py:108
Sparse Core Ops, SparseCore 0:
  68.1 32.3 all-gather.2
  107.5 34.9 all-gather.4
  152.2 45.9 reduce-scatter.1
where the time goes:
time: 281 us; the launch traced here: 280 us
  waiting for transfers between devices  104 us (37%)
  blocking collectives  87.7 us (31%)
  starting transfers between devices  33.7 us (12%)
  between operations  16.6 us (6%)
  other arithmetic  16.5 us (6%)
  matrix products  14.5 us (5%)
  local copies, waits for them, and re-layouts  7.14 us (3%)
    ppermute x4, waiting for transfers between devices, passed_along(): return lax.ppermute(value, axis, pairs)  51.1 us
    all_to_all x1, blocking collectives, body(): lax.all_to_all(pack(jnp.repeat(layer_in, TOP, axis=0)), 'expert', split_a...  50.4 us
    all_to_all x1, blocking collectives, body(): lax.all_to_all(pack((prob_flat[:, None] * repeated).astype(jnp.bfloat16))...  37.4 us
    all_gather x1, waiting for transfers between devices, body(): lax.all_gather(lax.all_to_all(pack((prob_flat[:, None] * repeated).astype...  29.3 us
    all_to_all x1, waiting for transfers between devices, body(): lax.all_to_all(summed.astype(jnp.bfloat16), 'expert', split_axis=0, conca...  20.8 us
    ppermute x4, starting transfers between devices, passed_along(): return lax.ppermute(value, axis, pairs)  17.2 us
    all_to_all x1, starting transfers between devices, body(): lax.all_to_all(summed.astype(jnp.bfloat16), 'expert', split_axis=0, conca...  16.4 us
  transfers between devices with their start and end apart: 8, of which 7 were waited for; matrix products, arithmetic and copies ran while one was open for 5% of the time, Pallas kernels for 0%

commit v1 on v0

--- a/solution.py
+++ b/solution.py
@@ -60,17 +60,25 @@
             axis=2,
             tiled=True,
         ),
-        lax.all_gather(
+        jnp.concatenate(
             lax.all_to_all(
-                pack((prob_flat[:, None] * repeated).astype(jnp.bfloat16)),
-                "expert",
-                split_axis=0,
-                concat_axis=0,
-                tiled=True,
+                jnp.stack(
+                    [
+                        lax.all_to_all(
+                            pack((prob_flat[:, None] * repeated).astype(jnp.bfloat16)),
+                            "expert",
+                            split_axis=0,
+                            concat_axis=0,
+                            tiled=True,
+                        )
+                    ]
+                    * lax.axis_size("dp")
+                ),
+                "dp",
+                0,
+                0,
             ),
-            "dp",
             axis=2,
-            tiled=True,
         ),
     )
     inputs = inputs.reshape(recv_rows, -1)

time: 281 us -> 304 us (1.082)
  blocking collectives: 87.7 us -> 142 us
  waiting for transfers between devices: 104 us -> 69.6 us
  local copies, waits for them, and re-layouts: 7.14 us -> 17 us
  starting transfers between devices: 33.7 us -> 28.3 us
    all_to_all x0 -> x1, blocking collectives: none -> 54.6 us  [body(): lax.all_to_all(jnp.stack([lax.all_to_all(pack((prob_flat[:, None] * repea...]
    all_gather x1 -> x0, waiting for transfers between devices: 29.3 us -> none  [body(): lax.all_gather(lax.all_to_all(pack((prob_flat[:, None] * repeated).astype...]
    all_to_all x1, waiting for transfers between devices: 20.8 us -> 5.28 us  [body(): lax.all_to_all(summed.astype(jnp.bfloat16), 'expert', split_axis=0, conca...]
    ppermute x4, waiting for transfers between devices: 51.1 us -> 64.3 us  [passed_along(): return lax.ppermute(value, axis, pairs)]
    unnamed x19 -> x18, local copies, waits for them, and re-layouts: 2.42 us -> 7.43 us
    all_to_all x1, starting transfers between devices: 16.4 us -> 11.5 us  [body(): lax.all_to_all(summed.astype(jnp.bfloat16), 'expert', split_axis=0, conca...]
    reshape x0 -> x1, local copies, waits for them, and re-layouts: none -> 4.54 us  [body(): jnp.concatenate(lax.all_to_all(jnp.stack([lax.all_to_all(pack((prob_flat[...]
  transfers between devices with their start and end apart: 8 -> 7, of which waited for: 7 -> 5; matrix products, arithmetic and copies ran while one was open for 5% -> 6% of each run, Pallas kernels for 0% -> 0%
where the time goes in v1:
time: 304 us; the launch traced here: 302 us
  blocking collectives  142 us (47%)
  waiting for transfers between devices  69.6 us (23%)
  starting transfers between devices  28.3 us (9%)
  local copies, waits for them, and re-layouts  17 us (6%)
  between operations  16.9 us (6%)
  other arithmetic  16.5 us (5%)
  matrix products  11.6 us (4%)
    ppermute x4, waiting for transfers between devices, passed_along(): return lax.ppermute(value, axis, pairs)  64.3 us
    all_to_all x1, blocking collectives, body(): lax.all_to_all(jnp.stack([lax.all_to_all(pack((prob_flat[:, None] * repea...  54.6 us
    all_to_all x1, blocking collectives, body(): lax.all_to_all(pack(jnp.repeat(layer_in, TOP, axis=0)), 'expert', split_a...  50.4 us
    all_to_all x1, blocking collectives, body(): lax.all_to_all(pack((prob_flat[:, None] * repeated).astype(jnp.bfloat16))...  37.3 us
    ppermute x4, starting transfers between devices, passed_along(): return lax.ppermute(value, axis, pairs)  16.8 us
    all_to_all x1, starting transfers between devices, body(): lax.all_to_all(summed.astype(jnp.bfloat16), 'expert', split_axis=0, conca...  11.5 us
    unnamed x18, local copies, waits for them, and re-layouts  7.43 us
  transfers between devices with their start and end apart: 7, of which 5 were waited for; matrix products, arithmetic and copies ran while one was open for 6% of the time, Pallas kernels for 0%

profile of v1, /device:TPU:6, one launch (start us, length us, event | category | flops | bytes accessed | tf_op | source)
XLA Modules:
  0.0 302.2 jit_solution(5225871049071796500)
XLA Ops:
  7.2 0.8 copy.25
  8.1 0.1 reshape.137
  8.2 0.1 reshape.136
  8.3 0.1 reshape.135
  8.4 1.2 slice.14
  9.6 1.3 fusion.41
  10.9 2.1 broadcast_compare_fusion
  13.0 0.8 select_reduce_fusion.1
  13.8 0.8 copy.24
  14.5 0.1 eq.98
  14.6 0.1 select_reduce_fusion
  14.7 0.6 reduce-window.6
  15.4 0.2 slice_reduce_fusion
  15.6 0.1 fusion.33
  15.7 1.9 scatter_custom_fusion
  17.6 50.4 %all_to_all.20 = bf16[64,8,512]{2,1,0:T(8,128)(2,1)} all-to-all(bf16[64,8,512]{2,1,0:T(8,128)(2,1)S(1)} %bitcast.75), channel_id=1, replica_groups=mesh['dp'=8,'expert'=64] {'expert'}, dimensions={0} | all-to-all | bytes 1048576 | tf_op jit(solution)/shard_map/all_to_all | solution.py:52
  68.2 0.1 mul.80
  68.3 1.7 scatter_custom_fusion.1
  70.0 37.3 %all_to_all.21 = bf16[64,8,512]{2,1,0:T(8,128)(2,1)S(1)} all-to-all(bf16[64,8,512]{2,1,0:T(8,128)(2,1)S(1)} %bitcast.76), channel_id=1, replica_groups=mesh['dp'=8,'expert'=64] {'expert'}, dimensions={0} | all-to-all | bytes 1048576 | tf_op jit(solution)/shard_map/all_to_all | solution.py:67
  107.3 0.4 stack.2
  107.6 54.6 %all_to_all.22 = bf16[8,64,8,512]{3,2,1,0:T(8,128)(2,1)S(1)} all-to-all(bf16[8,64,8,512]{3,2,1,0:T(8,128)(2,1)S(1)} %stack.2), channel_id=1, replica_groups=mesh['dp'=8,'expert'=64] {'dp'}, dimensions={0} | all-to-all | bytes 8388608 | tf_op jit(solution)/shard_map/all_to_all | solution.py:64
  162.2 4.5 %copy.35 = bf16[64,8,8,512]{3,2,1,0:T(8,128)(2,1)S(1)} copy(bf16[64,8,8,512]{3,1,0,2:T(8,128)(2,1)S(1)} %bitcast.74) | data formatting | bytes 8388608 | tf_op jit(solution)/shard_map/reshape | solution.py:63
  166.8 4.2 %copy.32 = bf16[64,8,8,512]{3,1,2,0:T(8,128)(2,1)} copy(bf16[64,8,8,512]{3,2,1,0:T(8,128)(2,1)S(1)} %copy.35) | data formatting | bytes 8388608
  171.0 3.6 %fusion.3 = f32[512,128]{1,0:T(8,128)S(1)} fusion(bf16[64,8,4096]{2,1,0:T(8,128)(2,1)} %all-gather.2.cloned.1.call-done, bf16[1,4096,128]{2,1,0:T(8,128)(2,1)S(1)} %copy-done), kind=kOutput, calls=%fused_computation.8 | convolution fusion | flops 536870912 | bytes 5505024 | tf_op jit(solution)/shard_map/dot_general | solution.py:90
  174.6 0.2 copy-done.2
  174.7 1.3 fusion.1
  176.0 0.9 copy-done.1
  176.9 0.8 convolution_convert_fusion
  177.7 0.4 copy-done.4
  178.1 1.3 fusion.10
  179.4 1.5 fusion.14
  180.9 3.2 %fusion = bf16[64,8,4096]{2,1,0:T(8,128)(2,1)} fusion(f32[512,4096]{1,0:T(8,128)S(1)} %fusion.14, bf16[1,4096,128]{2,1,0:T(8,128)(2,1)S(1)} %copy-done.3, f32[512,128]{1,0:T(8,128)S(1)} %fusion.10, f32[512,128]{1,0:T(8,128)S(1)} %fusion.3), kind=kOutput, calls=%fused_computation.4 | convolution fusion | flops 541458432 | bytes 14155776 | tf_op jit(solution)/shard_map/dot_general | solution.py:109
  184.2 3.3 %collective-permute-start = (bf16[128,4096]{1,0:T(8,128)(2,1)S(1)}, bf16[128,4096]{1,0:T(8,128)(2,1)S(1)}, u32[]{:S(2)}, u32[]{:S(2)}) collective-permute-start(bf16[128,4096]{1,0:T(8,128)(2,1)S(1)} %convolution_convert_fusion), channel_id=1, source_target_pairs={{0,1},{1,2},{2,3},{3,4},{4,5},{5,6},{6,7},{7,8},{8,9},{9,10},{10,1... | collective-permute-start | bytes 3145736 | tf_op jit(solution)/shard_map/ppermute | solution.py:12
  187.5 4.6 %collective-permute-start.2 = (bf16[128,4096]{1,0:T(8,128)(2,1)S(1)}, bf16[128,4096]{1,0:T(8,128)(2,1)}, u32[]{:S(2)}, u32[]{:S(2)}) collective-permute-start(bf16[128,4096]{1,0:T(8,128)(2,1)S(1)} %convolution_convert_fusion), channel_id=1, source_target_pairs={{0,63},{1,0},{2,1},{3,2},{4,3},{5,4},{6,5},{7,6},{8,7},{9,8},{10,9... | collective-permute-start | bytes 3145736 | tf_op jit(solution)/shard_map/ppermute | solution.py:12
  192.2 0.7 and_reduce_fusion.2
  194.2 18.5 %collective-permute-done = bf16[128,4096]{1,0:T(8,128)(2,1)S(1)} collective-permute-done((bf16[128,4096]{1,0:T(8,128)(2,1)S(1)}, bf16[128,4096]{1,0:T(8,128)(2,1)S(1)}, u32[]{:S(2)}, u32[]{:S(2)}) %collective-permute-start) | collective-permute-done | bytes 1048608 | tf_op jit(solution)/shard_map/ppermute | solution.py:12
  212.7 1.2 collective-permute-done.2
  213.9 3.2 %fusion.9 = (bf16[128,4096]{1,0:T(8,128)(2,1)}, bf16[128,4096]{1,0:T(8,128)(2,1)}) fusion(bf16[128,4096]{1,0:T(8,128)(2,1)S(1)} %collective-permute-done, bf16[128,4096]{1,0:T(8,128)(2,1)S(1)} %convolution_convert_fusion, f32[]{:T(128)S(6)} %convert_element_type.90, bf16[128,4096]{1,0:T(8,128)(2,1)} %collective-permute-done.2, f32[]{:T(128)S(6)} %convert_element_type.95), kind=kLoop, calls=%fused_computation.18 | loop fusion | flops 4718592 | bytes 5242888 | tf_op jit(solution)/shard_map/convert_element_type | solution.py:132
  217.1 2.7 collective-permute-start.1
  219.8 6.1 %collective-permute-start.3 = (bf16[128,4096]{1,0:T(8,128)(2,1)}, bf16[128,4096]{1,0:T(8,128)(2,1)}, u32[]{:S(2)}, u32[]{:S(2)}) collective-permute-start(bf16[128,4096]{1,0:T(8,128)(2,1)} %get-tuple-element.11), channel_id=1, source_target_pairs={{0,62},{1,63},{2,0},{3,1},{4,2},{5,3},{6,4},{7,5},{8,6},{9,7},{10,... | collective-permute-start | bytes 3145736 | tf_op jit(solution)/shard_map/ppermute | solution.py:12
  226.0 11.5 %all-to-all-start.3 = ((bf16[64,8,512]{2,1,0:T(8,128)(2,1)}), bf16[64,8,512]{2,1,0:T(8,128)(2,1)}, u32[]{:S(2)}, u32[]{:S(2)}) async-start(bf16[64,8,512]{2,1,0:T(8,128)(2,1)} %reduce-scatter.2.cloned.1.call-done), calls=%async_computation.4 | async-start | bytes 1048576 | tf_op jit(solution)/shard_map/all_to_all | solution.py:116
  238.7 39.7 %collective-permute-done.1 = bf16[128,4096]{1,0:T(8,128)(2,1)} collective-permute-done((bf16[128,4096]{1,0:T(8,128)(2,1)}, bf16[128,4096]{1,0:T(8,128)(2,1)}, u32[]{:S(2)}, u32[]{:S(2)}) %collective-permute-start.1) | collective-permute-done | bytes 1048608 | tf_op jit(solution)/shard_map/ppermute | solution.py:12
  278.4 4.9 %collective-permute-done.3 = bf16[128,4096]{1,0:T(8,128)(2,1)} collective-permute-done((bf16[128,4096]{1,0:T(8,128)(2,1)}, bf16[128,4096]{1,0:T(8,128)(2,1)}, u32[]{:S(2)}, u32[]{:S(2)}) %collective-permute-start.3) | collective-permute-done | bytes 1048608 | tf_op jit(solution)/shard_map/ppermute | solution.py:12
  283.3 3.9 %fusion.17 = bf16[1,128,4096]{2,1,0:T(8,128)(2,1)} fusion(bf16[128,4096]{1,0:T(8,128)(2,1)} %collective-permute-done.3, f32[]{:T(128)S(6)} %convert_element_type.97, bf16[128,4096]{1,0:T(8,128)(2,1)} %collective-permute-done.2, f32[]{:T(128)S(6)} %convert_element_type.95, bf16[128,4096]{1,0:T(8,128)(2,1)} %collective-permute-done.1, ...), kind=kLoop, calls=%fused_computation.26 | loop fusion | flops 8388608 | bytes 6291472 | tf_op jit(solution)/shard_map/broadcast_in_dim | solution.py:135
  287.2 5.3 %all-to-all-done.3 = bf16[64,8,512]{2,1,0:T(8,128)(2,1)} async-done(((bf16[64,8,512]{2,1,0:T(8,128)(2,1)}), bf16[64,8,512]{2,1,0:T(8,128)(2,1)}, u32[]{:S(2)}, u32[]{:S(2)}) %all-to-all-start.3) | async-done | bytes 524320 | tf_op jit(solution)/shard_map/all_to_all | solution.py:116
  292.5 1.2 bitcast_convert_fusion
  293.7 1.0 gather_fusion
  294.6 0.7 bitcast_reduce_fusion
  (26 shorter events, 0.3 us)
Async XLA Ops:
  7.2 163.8 %copy-start = (bf16[1,4096,128]{2,1,0:T(8,128)(2,1)S(1)}, bf16[1,4096,128]{2,1,0:T(8,128)(2,1)}, u32[]{:S(2)}) copy-start(bf16[1,4096,128]{2,1,0:T(8,128)(2,1)} %param.15) | copy-start | bytes 3145732
  7.2 60.9 %copy-start.5 = (bf16[32,512]{1,0:T(8,128)(2,1)S(1)}, bf16[32,512]{1,0:T(8,128)(2,1)}, u32[]{:S(2)}) copy-start(bf16[32,512]{1,0:T(8,128)(2,1)} %param.10) | copy-start | bytes 98308
  7.2 60.9 %copy-start.6 = (f32[32,8]{0,1:T(8,128)S(1)}, f32[32,8]{0,1:T(8,128)}, u32[]{:S(2)}) copy-start(f32[32,8]{0,1:T(8,128)} %param.11) | copy-start | bytes 3076
  7.2 163.8 %all-gather.2.cloned.1.call-start = ((), (), s32[]{:S(2)}) async-start(), calls=%async_computation.5 | async-start | bytes 4718592 | tf_op jit(solution)/shard_map/all_gather | solution.py:51
  68.0 157.9 %reduce-scatter.2.cloned.1.call-start = ((), (), s32[]{:S(2)}) async-start(), calls=%async_computation.6 | async-start | bytes 4718592 | tf_op jit(solution)/shard_map/reduce_scatter | solution.py:113
  171.0 3.6 %copy-start.3 = (bf16[1,4096,128]{2,1,0:T(8,128)(2,1)S(1)}, bf16[1,4096,128]{2,1,0:T(8,128)(2,1)}, u32[]{:S(2)}) copy-start(bf16[1,4096,128]{2,1,0:T(8,128)(2,1)} %param.16) | copy-start | bytes 3145732
  171.0 3.8 %copy-start.2 = (bf16[64,8,4096]{2,1,0:T(8,128)(2,1)S(1)}, bf16[64,8,4096]{2,1,0:T(8,128)(2,1)}, u32[]{:S(2)}) copy-start(bf16[64,8,4096]{2,1,0:T(8,128)(2,1)} %all-gather.2.cloned.1.call-done) | copy-start | bytes 12582916
  174.7 2.2 copy-start.1
  176.9 1.2 copy-start.4
  184.2 28.5 %collective-permute-start = (bf16[128,4096]{1,0:T(8,128)(2,1)S(1)}, bf16[128,4096]{1,0:T(8,128)(2,1)S(1)}, u32[]{:S(2)}, u32[]{:S(2)}) collective-permute-start(bf16[128,4096]{1,0:T(8,128)(2,1)S(1)} %convolution_convert_fusion), channel_id=1, source_target_pairs={{0,1},{1,2},{2,3},{3,4},{4,5},{5,6},{6,7},{7,8},{8,9},{9,10},{10,1... | collective-permute-start | bytes 3145736 | tf_op jit(solution)/shard_map/ppermute | solution.py:12
  187.5 26.4 %collective-permute-start.2 = (bf16[128,4096]{1,0:T(8,128)(2,1)S(1)}, bf16[128,4096]{1,0:T(8,128)(2,1)}, u32[]{:S(2)}, u32[]{:S(2)}) collective-permute-start(bf16[128,4096]{1,0:T(8,128)(2,1)S(1)} %convolution_convert_fusion), channel_id=1, source_target_pairs={{0,63},{1,0},{2,1},{3,2},{4,3},{5,4},{6,5},{7,6},{8,7},{9,8},{10,9... | collective-permute-start | bytes 3145736 | tf_op jit(solution)/shard_map/ppermute | solution.py:12
  217.1 61.3 %collective-permute-start.1 = (bf16[128,4096]{1,0:T(8,128)(2,1)}, bf16[128,4096]{1,0:T(8,128)(2,1)}, u32[]{:S(2)}, u32[]{:S(2)}) collective-permute-start(bf16[128,4096]{1,0:T(8,128)(2,1)} %get-tuple-element.10), channel_id=1, source_target_pairs={{0,2},{1,3},{2,4},{3,5},{4,6},{5,7},{6,8},{7,9},{8,10},{9,11},{10,... | collective-permute-start | bytes 3145736 | tf_op jit(solution)/shard_map/ppermute | solution.py:12
  219.8 63.5 %collective-permute-start.3 = (bf16[128,4096]{1,0:T(8,128)(2,1)}, bf16[128,4096]{1,0:T(8,128)(2,1)}, u32[]{:S(2)}, u32[]{:S(2)}) collective-permute-start(bf16[128,4096]{1,0:T(8,128)(2,1)} %get-tuple-element.11), channel_id=1, source_target_pairs={{0,62},{1,63},{2,0},{3,1},{4,2},{5,3},{6,4},{7,5},{8,6},{9,7},{10,... | collective-permute-start | bytes 3145736 | tf_op jit(solution)/shard_map/ppermute | solution.py:12
  226.0 66.5 %all-to-all-start.3 = ((bf16[64,8,512]{2,1,0:T(8,128)(2,1)}), bf16[64,8,512]{2,1,0:T(8,128)(2,1)}, u32[]{:S(2)}, u32[]{:S(2)}) async-start(bf16[64,8,512]{2,1,0:T(8,128)(2,1)} %reduce-scatter.2.cloned.1.call-done), calls=%async_computation.4 | async-start | bytes 1048576 | tf_op jit(solution)/shard_map/all_to_all | solution.py:116
Sparse Core Ops, SparseCore 0:
  68.1 32.3 all-gather.1
  184.3 36.7 reduce-scatter.1
